TPU v7x, 512 devices: a whole 4x8x8 slice. The times are simulated.
512 devices in a mesh: seq: 64 (over y, x, core), head: 8 (over z).
Axes of the slice: x: 4, y: 8, z: 8, core: 2. Of those that a mesh axis runs over, the one named last changes fastest.
Arguments:
- queries: bfloat16 [8192, 6144], P('seq', 'head'), may hold values from -6 to 6
- key_vectors: bfloat16 [8192, 6144], P('seq', 'head'), may hold values from -6 to 6
- value_vectors: bfloat16 [8192, 6144], P('seq', 'head'), may hold values from -6 to 6
- norm_gain: float32 [6144], P('head'), may hold values from 0.1 to 1.9
- upstream: bfloat16 [8192, 6144], P('seq', 'head'), may hold values from -6 to 6
Outputs:
- attended: bfloat16 [8192, 6144], P('seq', 'head')
- grad_queries: bfloat16 [8192, 6144], P('seq', 'head')
- grad_keys: bfloat16 [8192, 6144], P('seq', 'head')
- grad_values: bfloat16 [8192, 6144], P('seq', 'head')
- grad_gain: float32 [6144], P('head')
All inputs are finite; a program needn't handle non-finite values.
Results may differ from a plain program's by a relative error of at most 0.0058.
Values may be sent and summed in bfloat16 or wider, within the bound.
A program may use at most 64 MiB of HBM per device.

v0:
```python
import jax
import jax.numpy as jnp
from jax import lax
from jax.sharding import Mesh
from jax.sharding import PartitionSpec as P

HEADS = 48
HEAD_DIM = 128
SEQ = ("seq_0", "seq_1", "seq_2")


def cut_along(shard, dim, count):
    before, after = (shard.shape[:dim], shard.shape[dim + 1 :])
    return jnp.moveaxis(shard.reshape(*before, count, -1, *after), dim, 0)


def in_order(tiles, dim):
    tiles = jnp.moveaxis(tiles, 0, dim)
    shape = tiles.shape
    return tiles.reshape(*shape[:dim], shape[dim] * shape[dim + 1], *shape[dim + 2 :])


def moved_by_axis(tiles, axes, sequence):
    inside = tiles.shape[1:]
    out = tiles.reshape(*(lax.axis_size(a) for a in axes), *inside)
    for k in sequence:
        out = lax.all_to_all(out, axes[k], k, k, tiled=True)
    return out.reshape(-1, *inside)


def two_step_exchange(shard, groups, sequence, split_dim, concat_dim):
    count = lax.axis_size(groups[0]) * lax.axis_size(groups[1])
    tiles = cut_along(shard, split_dim, count)
    return in_order(moved_by_axis(tiles, groups, sequence), concat_dim)


def sent_to_all(shard, axis):
    count = lax.axis_size(axis)
    return lax.all_to_all(
        jnp.broadcast_to(shard[None], (count, *shard.shape)), axis, 0, 0, tiled=True
    )


def taken_together(shard, axis):
    everything = sent_to_all(shard, axis)
    return jnp.sum(everything, axis=0)


def packed_total(arrays, axis):
    ends = [0]
    for a in arrays:
        ends.append(ends[-1] + a.size)
    subtotal = taken_together(jnp.concatenate([a.ravel() for a in arrays]), axis)
    return tuple((subtotal[b:e].reshape(a.shape) for a, b, e in zip(arrays, ends, ends[1:])))


def split_shares(state):
    count = lax.axis_size(SEQ)
    return state.reshape(count, 1, -1)


def share_running(received, reverse):
    empty = jnp.zeros_like(received[:, :1])
    if reverse:
        summed = jnp.cumsum(received[:, ::-1], axis=1)[:, ::-1]
        return jnp.concatenate([summed[:, 1:], empty], axis=1)
    summed = jnp.cumsum(received, axis=1)
    return jnp.concatenate([empty, summed[:, :-1]], axis=1)


def body(queries, key_vectors, value_vectors, norm_gain, upstream):
    length = queries.shape[0]
    head_count = queries.shape[1] // HEAD_DIM
    total_width = HEADS * HEAD_DIM
    shaped = (length, head_count, HEAD_DIM)
    query_rows = queries.reshape(shaped)
    key_rows = key_vectors.reshape(shaped)
    value_rows = value_vectors.reshape(shaped)
    upstream_f = upstream.reshape(shaped).astype(jnp.float32)
    gain_grid = norm_gain.reshape(head_count, HEAD_DIM)
    positions = jnp.arange(length, dtype=jnp.int32)
    causal = (positions[None, :] <= positions[:, None])[None]
    local_state = jnp.einsum(
        "thd,the->hde", key_rows, value_rows, preferred_element_type=jnp.float32
    )
    moved = lax.all_to_all(split_shares(local_state), SEQ, split_axis=0, concat_axis=1, tiled=True)
    rounded = share_running(moved, False).astype(jnp.bfloat16)
    returned = two_step_exchange(rounded, (("seq_0", "seq_1"), "seq_2"), (1, 0), 1, 0)
    prior_b = returned.reshape(local_state.shape)
    scores = jnp.einsum("thd,shd->hts", query_rows, key_rows, preferred_element_type=jnp.float32)
    weights = jnp.where(causal, scores, 0.0).astype(jnp.bfloat16)
    out = jnp.einsum("hts,she->the", weights, value_rows, preferred_element_type=jnp.float32)
    out = out + jnp.einsum("thd,hde->the", query_rows, prior_b, preferred_element_type=jnp.float32)
    grad_norm = upstream_f * gain_grid
    square_total, cross_total = packed_total(
        (jnp.sum(out * out, axis=(1, 2)), jnp.sum(grad_norm * out, axis=(1, 2))), "head"
    )
    inv = lax.rsqrt(square_total / total_width + 1e-06)[:, None, None]
    scaled = out * inv
    mean_dot = cross_total[:, None, None] * inv / total_width
    attended = (scaled * gain_grid).astype(jnp.bfloat16).reshape(length, -1)
    d_out = (inv * (grad_norm - scaled * mean_dot)).astype(jnp.bfloat16)
    gain_part = jnp.sum(upstream_f * scaled, axis=0).reshape(-1)
    grad_state = jnp.einsum("thd,the->hde", query_rows, d_out, preferred_element_type=jnp.float32)
    moved_grad = lax.all_to_all(
        split_shares(grad_state), SEQ, split_axis=0, concat_axis=1, tiled=True
    )
    rounded_grad = share_running(moved_grad, True).astype(jnp.bfloat16)
    returned_grad = lax.all_to_all(rounded_grad, SEQ, split_axis=1, concat_axis=0, tiled=True)
    later_b = returned_grad.reshape(grad_state.shape)
    grad_gain = taken_together(gain_part, SEQ)
    d_scores = jnp.einsum("the,she->hts", d_out, value_rows, preferred_element_type=jnp.float32)
    d_scores = jnp.where(causal, d_scores, 0.0).astype(jnp.bfloat16)
    grad_q = jnp.einsum("hts,shd->thd", d_scores, key_rows, preferred_element_type=jnp.float32)
    grad_q = grad_q + jnp.einsum("the,hde->thd", d_out, prior_b, preferred_element_type=jnp.float32)
    grad_k = jnp.einsum("hts,thd->shd", d_scores, query_rows, preferred_element_type=jnp.float32)
    grad_k = grad_k + jnp.einsum(
        "she,hde->shd", value_rows, later_b, preferred_element_type=jnp.float32
    )
    grad_v = jnp.einsum("hts,the->she", weights, d_out, preferred_element_type=jnp.float32)
    grad_v = grad_v + jnp.einsum(
        "shd,hde->she", key_rows, later_b, preferred_element_type=jnp.float32
    )
    return (
        attended,
        grad_q.astype(jnp.bfloat16).reshape(length, -1),
        grad_k.astype(jnp.bfloat16).reshape(length, -1),
        grad_v.astype(jnp.bfloat16).reshape(length, -1),
        grad_gain,
    )


def solution(mesh):
    split = Mesh(
        mesh.devices.reshape(8, 4, 2, mesh.shape["head"]), ("seq_0", "seq_1", "seq_2", "head")
    )
    return jax.shard_map(
        body,
        mesh=split,
        in_specs=(P(SEQ, "head"), P(SEQ, "head"), P(SEQ, "head"), P("head"), P(SEQ, "head")),
        out_specs=(P(SEQ, "head"), P(SEQ, "head"), P(SEQ, "head"), P(SEQ, "head"), P("head")),
        check_vma=False,
    )
```

profile of v0, /device:TPU:1, one launch (start us, length us, event | category | flops | bytes accessed | tf_op | source)
XLA Modules:
  0.0 130.9 jit_solution(414153569281648489)
XLA Ops:
  0.6 1.1 copy.137
  1.9 1.0 fusion.8
  2.9 11.7 %all-to-all-start = ((f32[64,1,1536]{2,1,0:T(1,128)}), f32[64,1,1536]{2,1,0:T(1,128)S(1)}, u32[]{:S(2)}, u32[]{:S(2)}) async-start(f32[64,1,1536]{2,1,0:T(1,128)} %bitcast.4), calls=%async_computation | async-start | bytes 786432 | tf_op jit(solution)/shard_map/all_to_all | solution.py:86
  14.9 0.8 copy-done.2
  15.8 14.1 %all-to-all-done = f32[64,1,1536]{2,1,0:T(1,128)S(1)} async-done(((f32[64,1,1536]{2,1,0:T(1,128)}), f32[64,1,1536]{2,1,0:T(1,128)S(1)}, u32[]{:S(2)}, u32[]{:S(2)}) %all-to-all-start) | async-done | bytes 393248 | tf_op jit(solution)/shard_map/all_to_all | solution.py:86
  29.9 0.4 reduce_window_sum.17
  30.4 3.8 %all_to_all.55 = bf16[32,2,1,1,1536]{4,0,3,2,1:T(8,128)(2,1)S(1)} all-to-all(bf16[32,2,1,1,1536]{4,0,3,2,1:T(8,128)(2,1)S(1)} %copy.144), channel_id=1, replica_groups=mesh['seq_0'=8,'seq_1'=4,'seq_2'=2,'head'=8] {'seq_2'}, dimensions={1} | all-to-all | bytes 393216 | tf_op jit(solution)/shard_map/all_to_all | solution.py:27
  34.2 0.9 copy.145
  35.1 4.7 %all-to-all-start.2 = ((bf16[32,2,1,1,1536]{4,1,3,2,0:T(2,128)(2,1)}), bf16[32,2,1,1,1536]{4,1,3,2,0:T(2,128)(2,1)S(1)}, u32[]{:S(2)}, u32[]{:S(2)}) async-start(bf16[32,2,1,1,1536]{4,1,3,2,0:T(2,128)(2,1)} %copy.145), calls=%async_computation.2 | async-start | bytes 393216 | tf_op jit(solution)/shard_map/all_to_all | solution.py:27
  40.4 10.1 %all-to-all-done.2 = bf16[32,2,1,1,1536]{4,1,3,2,0:T(2,128)(2,1)S(1)} async-done(((bf16[32,2,1,1,1536]{4,1,3,2,0:T(2,128)(2,1)}), bf16[32,2,1,1,1536]{4,1,3,2,0:T(2,128)(2,1)S(1)}, u32[]{:S(2)}, u32[]{:S(2)}) %all-to-all-start.2) | async-done | bytes 196640 | tf_op jit(solution)/shard_map/all_to_all | solution.py:27
  50.5 0.6 copy-done.3
  51.5 16.4 %all_to_all.56 = f32[8,1,256]{2,1,0:T(1,128)S(1)} all-to-all(f32[8,1,256]{2,1,0:T(1,128)S(1)} %broadcast_in_dim.38), channel_id=1, replica_groups=mesh['seq_0'=8,'seq_1'=4,'seq_2'=2,'head'=8] {'head'}, dimensions={0} | all-to-all | bytes 16384 | tf_op jit(solution)/shard_map/all_to_all | solution.py:39
  68.5 0.9 copy.154
  69.4 7.5 %all-to-all-start.4 = ((f32[64,1,1536]{2,1,0:T(1,128)}), f32[64,1,1536]{2,1,0:T(1,128)S(1)}, u32[]{:S(2)}, u32[]{:S(2)}) async-start(f32[64,1,1536]{2,1,0:T(1,128)} %bitcast.15), calls=%async_computation.4 | async-start | bytes 786432 | tf_op jit(solution)/shard_map/all_to_all | solution.py:105
  77.1 15.1 %all-to-all-done.4 = f32[64,1,1536]{2,1,0:T(1,128)S(1)} async-done(((f32[64,1,1536]{2,1,0:T(1,128)}), f32[64,1,1536]{2,1,0:T(1,128)S(1)}, u32[]{:S(2)}, u32[]{:S(2)}) %all-to-all-start.4) | async-done | bytes 393248 | tf_op jit(solution)/shard_map/all_to_all | solution.py:105
  92.2 0.8 broadcast_in_dim.40
  93.0 5.4 %all-to-all-start.6 = ((f32[64,1,768]{2,1,0:T(1,128)}), f32[64,1,768]{2,1,0:T(1,128)S(1)}, u32[]{:S(2)}, u32[]{:S(2)}) async-start(f32[64,1,768]{2,1,0:T(1,128)} %broadcast_in_dim.40), calls=%async_computation.6 | async-start | bytes 393216 | tf_op jit(solution)/shard_map/all_to_all | solution.py:39
  98.7 0.4 reduce_window_sum.18
  99.1 0.5 slice.20
  99.9 0.4 pad_bitcast_fusion
  100.3 0.5 broadcast.22
  100.8 1.8 %reduce.4 = bf16[64,1536]{1,0:T(8,128)(2,1)S(1)} reduce(bf16[64,1,1536]{2,1,0:T(2,128)(2,1)S(1)} %pad_bitcast_fusion, bf16[]{:T(256)} %broadcast.22), dimensions={1}, to_apply=%pad_bitcast_fusion.reduce_sub_computation | reduce | bytes 393218
  102.6 0.7 reshape.96
  103.4 7.0 %all-to-all-done.6 = f32[64,1,768]{2,1,0:T(1,128)S(1)} async-done(((f32[64,1,768]{2,1,0:T(1,128)}), f32[64,1,768]{2,1,0:T(1,128)S(1)}, u32[]{:S(2)}, u32[]{:S(2)}) %all-to-all-start.6) | async-done | bytes 196640 | tf_op jit(solution)/shard_map/all_to_all | solution.py:39
  110.4 4.5 %all-to-all-start.5 = ((bf16[64,2,768]{2,1,0:T(2,128)(2,1)}), bf16[64,2,768]{2,1,0:T(2,128)(2,1)S(1)}, u32[]{:S(2)}, u32[]{:S(2)}) async-start(bf16[64,2,768]{2,1,0:T(2,128)(2,1)} %reshape.96), calls=%async_computation.5 | async-start | bytes 393216 | tf_op jit(solution)/shard_map/all_to_all | solution.py:109
  115.1 0.8 copy.163
  115.9 0.8 copy.162
  116.9 0.7 reduce_sum.49
  117.7 9.4 %all-to-all-done.5 = bf16[64,2,768]{2,1,0:T(2,128)(2,1)S(1)} async-done(((bf16[64,2,768]{2,1,0:T(2,128)(2,1)}), bf16[64,2,768]{2,1,0:T(2,128)(2,1)S(1)}, u32[]{:S(2)}, u32[]{:S(2)}) %all-to-all-start.5) | async-done | bytes 196640 | tf_op jit(solution)/shard_map/all_to_all | solution.py:109
  127.2 1.1 bitcast_reduce_fusion
  129.0 0.8 copy.165
  130.1 0.8 copy.164
  (36 shorter events, 4.6 us)
Async XLA Ops:
  0.6 1.1 copy-start
  2.9 11.8 %copy-start.1 = (bf16[128,768]{1,0:T(8,128)(2,1)S(1)}, bf16[128,768]{1,0:T(8,128)(2,1)}, u32[]{:S(2)}) copy-start(bf16[128,768]{1,0:T(8,128)(2,1)} %param.5) | copy-start | bytes 589828
  2.9 26.9 %all-to-all-start = ((f32[64,1,1536]{2,1,0:T(1,128)}), f32[64,1,1536]{2,1,0:T(1,128)S(1)}, u32[]{:S(2)}, u32[]{:S(2)}) async-start(f32[64,1,1536]{2,1,0:T(1,128)} %bitcast.4), calls=%async_computation | async-start | bytes 786432 | tf_op jit(solution)/shard_map/all_to_all | solution.py:86
  14.7 0.9 copy-start.2
  35.1 15.3 %all-to-all-start.2 = ((bf16[32,2,1,1,1536]{4,1,3,2,0:T(2,128)(2,1)}), bf16[32,2,1,1,1536]{4,1,3,2,0:T(2,128)(2,1)S(1)}, u32[]{:S(2)}, u32[]{:S(2)}) async-start(bf16[32,2,1,1,1536]{4,1,3,2,0:T(2,128)(2,1)} %copy.145), calls=%async_computation.2 | async-start | bytes 393216 | tf_op jit(solution)/shard_map/all_to_all | solution.py:27
  50.4 0.7 copy-start.3
  69.4 22.8 %all-to-all-start.4 = ((f32[64,1,1536]{2,1,0:T(1,128)}), f32[64,1,1536]{2,1,0:T(1,128)S(1)}, u32[]{:S(2)}, u32[]{:S(2)}) async-start(f32[64,1,1536]{2,1,0:T(1,128)} %bitcast.15), calls=%async_computation.4 | async-start | bytes 786432 | tf_op jit(solution)/shard_map/all_to_all | solution.py:105
  93.0 17.4 %all-to-all-start.6 = ((f32[64,1,768]{2,1,0:T(1,128)}), f32[64,1,768]{2,1,0:T(1,128)S(1)}, u32[]{:S(2)}, u32[]{:S(2)}) async-start(f32[64,1,768]{2,1,0:T(1,128)} %broadcast_in_dim.40), calls=%async_computation.6 | async-start | bytes 393216 | tf_op jit(solution)/shard_map/all_to_all | solution.py:39
  110.4 16.7 %all-to-all-start.5 = ((bf16[64,2,768]{2,1,0:T(2,128)(2,1)}), bf16[64,2,768]{2,1,0:T(2,128)(2,1)S(1)}, u32[]{:S(2)}, u32[]{:S(2)}) async-start(bf16[64,2,768]{2,1,0:T(2,128)(2,1)} %reshape.96), calls=%async_computation.5 | async-start | bytes 393216 | tf_op jit(solution)/shard_map/all_to_all | solution.py:109
where the time goes:
time: 132 us; the launch traced here: 131 us
  waiting for transfers between devices  55.6 us (42%)
  starting transfers between devices  33.8 us (26%)
  blocking collectives  20.2 us (15%)
  local copies, waits for them, and re-layouts  13.1 us (10%)
  matrix products  3.66 us (3%)
  other arithmetic  3.62 us (3%)
    all_to_all x1, blocking collectives, sent_to_all(): lax.all_to_all(jnp.broadcast_to(shard[None], (count, *shard.shape)), axis...  16.4 us
    all_to_all x1, waiting for transfers between devices, body(): lax.all_to_all(split_shares(grad_state), SEQ, split_axis=0, concat_axis=1...  15.1 us
    all_to_all x1, waiting for transfers between devices, body(): lax.all_to_all(split_shares(local_state), SEQ, split_axis=0, concat_axis=...  14.1 us
    all_to_all x1, starting transfers between devices, body(): lax.all_to_all(split_shares(local_state), SEQ, split_axis=0, concat_axis=...  11.7 us
    all_to_all x1, waiting for transfers between devices, moved_by_axis(): out = lax.all_to_all(out, axes[k], k, k, tiled=True)  10.1 us
    all_to_all x1, waiting for transfers between devices, body(): lax.all_to_all(rounded_grad, SEQ, split_axis=1, concat_axis=0, tiled=True)  9.42 us
    unnamed x20, local copies, waits for them, and re-layouts  8.16 us
    all_to_all x1, starting transfers between devices, body(): lax.all_to_all(split_shares(grad_state), SEQ, split_axis=0, concat_axis=1...  7.46 us
  transfers between devices with their start and end apart: 5, of which 5 were waited for; matrix products, arithmetic and copies ran while one was open for 7% of the time, Pallas kernels for 0%

commit v1 on v0

v1 whole, which is shorter than its diff:
```python
import jax
import jax.numpy as jnp
from jax import lax
from jax.experimental import pallas as pl
from jax.experimental.pallas import tpu as pltpu
from jax.sharding import PartitionSpec as P

HEADS = 48
D = 128
BF = jnp.bfloat16
F32 = jnp.float32
GROUP = 16
GROUP_ORDER = (12, 13, 4, 5, 10, 11, 14, 15, 8, 9, 2, 3, 6, 7, 1)
CROSS = (56, 40, 16)
COLUMN = (32, 40, 24, 56, 16, 48, 8)
ROW = (4, 5, 2, 3, 6, 7, 1)
DEPTH = (4, 3, 5, 2, 6, 1, 7)


def nn(a, b):
    return lax.dot_general(a, b, (((1,), (0,)), ((), ())), preferred_element_type=F32)


def nt(a, b):
    return lax.dot_general(a, b, (((1,), (1,)), ((), ())), preferred_element_type=F32)


def tn(a, b):
    return lax.dot_general(a, b, (((0,), (0,)), ((), ())), preferred_element_type=F32)


def kernel(
    q_hbm, k_hbm, v_hbm, g_hbm, u_hbm,
    at_hbm, gq_hbm, gk_hbm, gv_hbm, gg_hbm,
    q, k, v, g, u, at, gq, gk, gv, gg,
    w, part, out, d_out, keys, vals,
    state, moved, run, total, others, back, whole,
    state2, moved2, run2, total2, others2, back2, whole2,
    norm, norms, gain, gains, gain2, gains2,
    in_sem, out_sem,
    rs_s, rs_r, ex_s, ex_r, ag_s, ag_r,
    rs2_s, rs2_r, ex2_s, ex2_r, ag2_s, ag2_r,
    nm_s, nm_r, c_s, c_r, r_s, r_r,
):
    heads = q_hbm.shape[1] // D
    length = q_hbm.shape[0]
    seq = lax.axis_index("seq")
    head = lax.axis_index("head")
    inner = seq & 15
    outer = seq >> 4
    share = inner ^ ((seq >> 2) & 8)

    loads = [
        pltpu.make_async_copy(a, b, in_sem.at[i])
        for i, (a, b) in enumerate(((k_hbm, k), (v_hbm, v), (q_hbm, q), (u_hbm, u), (g_hbm, g)))
    ]
    for c in loads:
        c.start()

    barrier = pltpu.get_barrier_semaphore()
    peers = sorted(set(GROUP_ORDER) | set(CROSS) | set(COLUMN))
    for m in peers:
        pl.semaphore_signal(barrier, inc=1, device_id={"seq": seq ^ m}, device_id_type=pl.DeviceIdType.MESH)
    for m in DEPTH:
        pl.semaphore_signal(barrier, inc=1, device_id={"head": head ^ m}, device_id_type=pl.DeviceIdType.MESH)

    def send(src, dst, s, r, **where):
        c = pltpu.make_async_remote_copy(
            src_ref=src, dst_ref=dst, send_sem=s, recv_sem=r,
            device_id=where, device_id_type=pl.DeviceIdType.MESH,
        )
        c.start()
        return c

    def cols(h):
        return slice(h * D, (h + 1) * D)

    def scatter(state_ref, moved_ref, s, r):
        copies = []
        for m in GROUP_ORDER:
            copies.append(send(state_ref.at[share ^ m], moved_ref.at[m], s.at[m], r.at[m], seq=seq ^ m))
        moved_ref[0] = state_ref[share]
        return copies

    def cross(copies, moved_ref, total_ref, others_ref, s, r):
        for c in copies:
            c.wait_recv()
        acc = moved_ref[0].astype(F32)
        for m in range(1, GROUP):
            acc = acc + moved_ref[m].astype(F32)
        total_ref[...] = acc.astype(BF)
        return [
            send(total_ref, others_ref.at[i], s.at[i], r.at[i], seq=seq ^ m)
            for i, m in enumerate(CROSS)
        ]

    def running(moved_ref, run_ref, reverse):
        acc = jnp.zeros(run_ref.shape[1:], F32)
        order = range(GROUP - 1, -1, -1) if reverse else range(GROUP)
        for i in order:
            slot = inner ^ i
            run_ref[slot] = acc
            acc = acc + moved_ref[slot].astype(F32)

    def gather(copies, run_ref, others_ref, back_ref, whole_ref, s, r, reverse):
        for c in copies:
            c.wait_recv()
        base = jnp.zeros(run_ref.shape[1:], F32)
        for i, m in enumerate(CROSS):
            peer = outer ^ (m >> 4)
            take = (peer > outer) if reverse else (peer < outer)
            base = base + jnp.where(take, others_ref[i].astype(F32), 0.0)
        sent = []
        for m in GROUP_ORDER:
            back_ref[m] = (run_ref[m] + base).astype(BF)
            sent.append(send(back_ref.at[m], whole_ref.at[share], s.at[m], r.at[m], seq=seq ^ m))
        whole_ref[share] = (run_ref[0] + base).astype(BF)
        return sent

    pend = []
    loads[0].wait()
    loads[1].wait()
    for h in range(heads):
        keys[h * D:(h + 1) * D] = tn(k[:, cols(h)], v[:, cols(h)])
    state[...] = keys[...].astype(BF).reshape(state.shape)
    pl.semaphore_wait(barrier, len(peers) + len(DEPTH))
    first = scatter(state, moved, rs_s, rs_r)
    pend += first

    rows = lax.broadcasted_iota(jnp.int32, (length, length), 0)
    columns = lax.broadcasted_iota(jnp.int32, (length, length), 1)
    causal = columns <= rows
    loads[2].wait()
    for h in range(heads):
        scores = nt(q[:, cols(h)], k[:, cols(h)])
        wh = jnp.where(causal, scores, 0.0).astype(BF)
        w[:, cols(h)] = wh
        part[:, cols(h)] = nn(wh, v[:, cols(h)])
    loads[3].wait()
    loads[4].wait()

    second = cross(first, moved, total, others, ex_s, ex_r)
    pend += second
    running(moved, run, False)
    third = gather(second, run, others, back, whole, ag_s, ag_r, False)
    pend += third
    for c in third:
        c.wait_recv()

    prior = whole[...].reshape(heads * D, D)
    squares = jnp.zeros((length, D), F32)
    crosses = jnp.zeros((length, D), F32)
    for h in range(heads):
        o = part[:, cols(h)] + nn(q[:, cols(h)], prior[h * D:(h + 1) * D])
        out[:, cols(h)] = o
        grad_norm = u[:, cols(h)].astype(F32) * g[pl.ds(h * D, D)][None, :]
        squares = squares + o * o
        crosses = crosses + grad_norm * o
    norm[0:1, :] = jnp.sum(squares.T, axis=0, keepdims=True)
    norm[1:2, :] = jnp.sum(crosses.T, axis=0, keepdims=True)
    fourth = [
        send(norm, norms.at[i], nm_s.at[i], nm_r.at[i], head=head ^ m) for i, m in enumerate(DEPTH)
    ]
    pend += fourth
    for c in fourth:
        c.wait_recv()
    sums = norm[...]
    for i in range(len(DEPTH)):
        sums = sums + norms[i]
    width = HEADS * D
    inv_row = lax.rsqrt(sums[0:1] / width + 1e-06)
    mean_row = sums[1:2] * inv_row / width
    inv = jnp.broadcast_to(inv_row, (D, length)).T
    mean = jnp.broadcast_to(mean_row, (D, length)).T

    for h in range(heads):
        scaled = out[:, cols(h)] * inv
        gh = g[pl.ds(h * D, D)][None, :]
        uf = u[:, cols(h)].astype(F32)
        dh = (inv * (uf * gh - scaled * mean)).astype(BF)
        d_out[:, cols(h)] = dh
        at[:, cols(h)] = (scaled * gh).astype(BF)
        gain[h:h + 1, :] = jnp.sum(uf * scaled, axis=0, keepdims=True)
        keys[h * D:(h + 1) * D] = tn(q[:, cols(h)], dh)
    state2[...] = keys[...].astype(BF).reshape(state2.shape)
    first = scatter(state2, moved2, rs2_s, rs2_r)
    pend += first
    fifth = [
        send(gain, gains.at[i], c_s.at[i], c_r.at[i], seq=seq ^ m) for i, m in enumerate(COLUMN)
    ]
    pend += fifth
    stores = [pltpu.make_async_copy(at, at_hbm, out_sem.at[0])]
    stores[-1].start()

    for h in range(heads):
        dh = d_out[:, cols(h)]
        scores = nt(dh, v[:, cols(h)])
        ds = jnp.where(causal, scores, 0.0).astype(BF)
        part[:, cols(h)] = tn(ds, q[:, cols(h)])
        gq[:, cols(h)] = (nn(ds, k[:, cols(h)]) + nt(dh, prior[h * D:(h + 1) * D])).astype(BF)
    stores.append(pltpu.make_async_copy(gq, gq_hbm, out_sem.at[1]))
    stores[-1].start()

    second = cross(first, moved2, total2, others2, ex2_s, ex2_r)
    pend += second
    running(moved2, run2, True)
    for c in fifth:
        c.wait_recv()
    column = gain[...]
    for i in range(len(COLUMN)):
        column = column + gains[i]
    gain2[...] = column
    sixth = [
        send(gain2, gains2.at[i], r_s.at[i], r_r.at[i], seq=seq ^ m) for i, m in enumerate(ROW)
    ]
    pend += sixth
    third = gather(second, run2, others2, back2, whole2, ag2_s, ag2_r, True)
    pend += third
    for h in range(heads):
        vals[:, cols(h)] = tn(w[:, cols(h)], d_out[:, cols(h)])
    for c in sixth:
        c.wait_recv()
    column = gain2[...]
    for i in range(len(ROW)):
        column = column + gains2[i]
    for h in range(heads):
        gg[pl.ds(h * D, D)] = column[h]
    stores.append(pltpu.make_async_copy(gg, gg_hbm, out_sem.at[2]))
    stores[-1].start()
    for c in third:
        c.wait_recv()
    later = whole2[...].reshape(heads * D, D)
    for h in range(heads):
        lh = later[h * D:(h + 1) * D]
        gk[:, cols(h)] = (part[:, cols(h)] + nt(v[:, cols(h)], lh)).astype(BF)
    stores.append(pltpu.make_async_copy(gk, gk_hbm, out_sem.at[3]))
    stores[-1].start()
    for h in range(heads):
        lh = later[h * D:(h + 1) * D]
        gv[:, cols(h)] = (vals[:, cols(h)] + nn(k[:, cols(h)], lh)).astype(BF)
    stores.append(pltpu.make_async_copy(gv, gv_hbm, out_sem.at[4]))
    stores[-1].start()
    for c in pend:
        c.wait_send()
    for c in stores:
        c.wait()


def body(queries, key_vectors, value_vectors, norm_gain, upstream):
    length, width = queries.shape
    heads = width // D
    rows = heads * D // GROUP
    tall = jax.ShapeDtypeStruct((length, width), BF)
    sem = pltpu.SemaphoreType.DMA

    def scan_buffers():
        return [
            pltpu.VMEM((GROUP, rows, D), BF),
            pltpu.VMEM((GROUP, rows, D), BF),
            pltpu.VMEM((GROUP, rows, D), F32),
            pltpu.VMEM((rows, D), BF),
            pltpu.VMEM((3, rows, D), BF),
            pltpu.VMEM((GROUP, rows, D), BF),
            pltpu.VMEM((GROUP, rows, D), BF),
        ]

    def scan_sems():
        return [sem((GROUP,)), sem((GROUP,)), sem((3,)), sem((3,)), sem((GROUP,)), sem((GROUP,))]

    return pl.pallas_call(
        kernel,
        out_shape=(tall, tall, tall, tall, jax.ShapeDtypeStruct((width,), F32)),
        in_specs=[pl.BlockSpec(memory_space=pl.ANY)] * 5,
        out_specs=[pl.BlockSpec(memory_space=pl.ANY)] * 5,
        scratch_shapes=[
            pltpu.VMEM((length, width), BF),
            pltpu.VMEM((length, width), BF),
            pltpu.VMEM((length, width), BF),
            pltpu.VMEM((width,), F32),
            pltpu.VMEM((length, width), BF),
            pltpu.VMEM((length, width), BF),
            pltpu.VMEM((length, width), BF),
            pltpu.VMEM((length, width), BF),
            pltpu.VMEM((length, width), BF),
            pltpu.VMEM((width,), F32),
            pltpu.VMEM((length, width), BF),
            pltpu.VMEM((length, width), F32),
            pltpu.VMEM((length, width), F32),
            pltpu.VMEM((length, width), BF),
            pltpu.VMEM((width, D), F32),
            pltpu.VMEM((length, width), F32),
            *scan_buffers(),
            *scan_buffers(),
            pltpu.VMEM((2, D), F32),
            pltpu.VMEM((7, 2, D), F32),
            pltpu.VMEM((heads, D), F32),
            pltpu.VMEM((7, heads, D), F32),
            pltpu.VMEM((heads, D), F32),
            pltpu.VMEM((7, heads, D), F32),
            sem((5,)),
            sem((5,)),
            *scan_sems(),
            *scan_sems(),
            sem((7,)), sem((7,)), sem((7,)), sem((7,)), sem((7,)), sem((7,)),
        ],
        compiler_params=pltpu.CompilerParams(collective_id=0, has_side_effects=True),
    )(queries, key_vectors, value_vectors, norm_gain, upstream)


def solution(mesh):
    tall = P("seq", "head")
    return jax.shard_map(
        body,
        mesh=mesh,
        in_specs=(tall, tall, tall, P("head"), tall),
        out_specs=(tall, tall, tall, tall, P("head")),
        check_vma=False,
    )
```

time: 132 us -> 54.4 us (0.41)
  waiting for transfers between devices: 55.6 us -> 0 us
  Pallas kernels: 0 us -> 48.5 us
  starting transfers between devices: 33.8 us -> 0 us
  blocking collectives: 20.2 us -> 0 us
  local copies, waits for them, and re-layouts: 13.1 us -> 4.93 us
  matrix products: 3.66 us -> 0 us
  other arithmetic: 3.62 us -> 0 us
    all_to_all x5 -> x0, waiting for transfers between devices: 55.6 us -> none  [the longest x1 15.1 us: body(): lax.all_to_all(split_shares(grad_state), SEQ, split_axis=0, concat_axis=1...]
    pallas_call x0 -> x1, Pallas kernels: none -> 48.5 us  [body(): pl.pallas_call(kernel, out_shape=(tall, tall, tall, tall, jax.ShapeDtypeS...]
    all_to_all x5 -> x0, starting transfers between devices: 33.8 us -> none  [the longest x1 11.7 us: body(): lax.all_to_all(split_shares(local_state), SEQ, split_axis=0, concat_axis=...]
    all_to_all x2 -> x0, blocking collectives: 20.2 us -> none  [the longest x1 16.4 us: sent_to_all(): lax.all_to_all(jnp.broadcast_to(shard[None], (count, *shard.shape)), axis...]
    dot_general x12 -> x0, matrix products: 3.66 us -> none  [the longest x1 1 us: body(): jnp.einsum('thd,the->hde', key_rows, value_rows, preferred_element_type=j...]
    unnamed x20 -> x13, local copies, waits for them, and re-layouts: 8.16 us -> 4.93 us
    all_to_all x3 -> x0, local copies, waits for them, and re-layouts: 1.99 us -> none  [the longest x1 1.08 us: body(): lax.all_to_all(rounded_grad, SEQ, split_axis=1, concat_axis=0, tiled=True)]
    unnamed x1 -> x0, other arithmetic: 1.79 us -> none
  transfers between devices with their start and end apart: 5 -> 0, of which waited for: 5 -> 0; matrix products, arithmetic and copies ran while one was open for 7% -> 0% of each run, Pallas kernels for 0% -> 0%
where the time goes in v1:
time: 54.4 us; the launch traced here: 54.1 us
  Pallas kernels  48.5 us (89%)
  local copies, waits for them, and re-layouts  4.93 us (9%)
  between operations  0.65 us (1%)
    pallas_call x1, Pallas kernels, body(): pl.pallas_call(kernel, out_shape=(tall, tall, tall, tall, jax.ShapeDtypeS...  48.5 us
    unnamed x13, local copies, waits for them, and re-layouts  4.93 us

profile of v1, /device:TPU:1, one launch (start us, length us, event | category | flops | bytes accessed | tf_op | source)
XLA Modules:
  0.0 54.1 jit_solution(2071690728557891005)
XLA Ops:
  0.6 48.5 %shard_map.92 = (bf16[128,768]{1,0:T(8,128)(2,1)}, bf16[128,768]{1,0:T(8,128)(2,1)}, bf16[128,768]{1,0:T(8,128)(2,1)}, bf16[128,768]{1,0:T(8,128)(2,1)}, f32[768]{0:T(1024)}) custom-call(bf16[128,768]{1,0:T(8,128)(2,1)} %q_hbm.1, bf16[128,768]{1,0:T(8,128)(2,1)} %k_hbm.1, bf16[128,768]{1,0:T(8,128)(2,1)} %v_hbm.1, f32[768]{0:T(1024)} %g_hbm.1, ...), custom_call_target="tpu_custom_call" | custom-call | tf_op jit(solution)/shard_map/pallas_call | solution.py:270
  49.2 0.0 copy-start.2
  49.2 1.7 %copy.15 = bf16[128,768]{1,0:T(8,128)(2,1)} copy(bf16[128,768]{1,0:T(8,128)(2,1)} %get-tuple-element.10) | data formatting | bytes 393216
  50.8 0.0 copy-done.2
  50.8 0.0 copy-start.1
  50.9 0.7 %copy.16 = bf16[128,768]{1,0:T(8,128)(2,1)} copy(bf16[128,768]{1,0:T(8,128)(2,1)S(1)} %copy-done.2) | data formatting | bytes 393216
  51.5 0.3 copy-done.1
  51.8 0.0 copy-start
  51.8 0.7 %copy.17 = bf16[128,768]{1,0:T(8,128)(2,1)} copy(bf16[128,768]{1,0:T(8,128)(2,1)S(1)} %copy-done.1) | data formatting | bytes 393216
  52.5 0.3 copy-done
  52.8 0.0 copy-start.3
  52.8 0.7 %copy.18 = bf16[128,768]{1,0:T(8,128)(2,1)} copy(bf16[128,768]{1,0:T(8,128)(2,1)S(1)} %copy-done) | data formatting | bytes 393216
  53.5 0.0 copy-done.3
  53.5 0.6 %copy.19 = f32[768]{0:T(1024)} copy(f32[768]{0:T(1024)S(1)} %copy-done.3) | data formatting | bytes 6144
Async XLA Ops:
  49.2 1.7 %copy-start.2 = (bf16[128,768]{1,0:T(8,128)(2,1)S(1)}, bf16[128,768]{1,0:T(8,128)(2,1)}, u32[]{:S(2)}) copy-start(bf16[128,768]{1,0:T(8,128)(2,1)} %get-tuple-element.11) | copy-start | bytes 589828
  50.8 1.0 %copy-start.1 = (bf16[128,768]{1,0:T(8,128)(2,1)S(1)}, bf16[128,768]{1,0:T(8,128)(2,1)}, u32[]{:S(2)}) copy-start(bf16[128,768]{1,0:T(8,128)(2,1)} %get-tuple-element.12) | copy-start | bytes 589828
  51.8 1.0 %copy-start = (bf16[128,768]{1,0:T(8,128)(2,1)S(1)}, bf16[128,768]{1,0:T(8,128)(2,1)}, u32[]{:S(2)}) copy-start(bf16[128,768]{1,0:T(8,128)(2,1)} %get-tuple-element.13) | copy-start | bytes 589828
  52.8 0.7 %copy-start.3 = (f32[768]{0:T(1024)S(1)}, f32[768]{0:T(1024)}, u32[]{:S(2)}) copy-start(f32[768]{0:T(1024)} %get-tuple-element.14) | copy-start | bytes 9220
